TPU v7x, 256 devices: a whole 4x4x8 slice. The times are simulated.
256 devices in a mesh: blk: 32 (over z, y), view: 8 (over x, core).
Axes of the slice: x: 4, y: 4, z: 8, core: 2. Of those that a mesh axis runs over, the one named last changes fastest.
Arguments:
- estimate: float32 [512, 128, 256], P('blk'), may hold values from 0.3 to 3
- views: float32 [8, 512, 128, 256], P('view', 'blk'), may hold values from 0.3 to 3
- axial_taps: float32 [8, 33], P('view'), may hold values from 0.1 to 1
- lateral_taps: float32 [8, 2, 17], P('view'), may hold values from 0.05 to 1
- cover: int32 [8, 2], P('view'), may hold values from 0 to 512, as said below
Outputs:
- refined: float32 [512, 128, 256], P('blk')
Inputs may be any that keep to these rules, and one draw needn't show every extreme that they name: cover[v, 0] < cover[v, 1]; every first plane is at most 128 and every end at least 384; some view starts at plane 0 and some view ends at 512.
All inputs are finite; a program needn't handle non-finite values.
Results may differ from a plain program's by a relative error of at most 0.00015.
Values sent between devices are 32-bit elements; how exact they have to be, the bound alone decides.
No kernel may reach another device: no remote copies, remote signals or barrier semaphores. Data moves between devices by JAX's collectives and lax.ppermute only.
A program may use at most 64 MiB of HBM per device.

v0:
```python
import jax
import jax.numpy as jnp
from jax import lax
from jax.sharding import PartitionSpec as P

RAD = 8
RZ = 16
ITERS = 2


def padded(block, sides, width):
    for axis, dim in sides:
        count = lax.axis_size(axis)
        forward = [(i, i + 1) for i in range(count - 1)]
        backward = [(target, source) for source, target in forward]
        low = lax.ppermute(
            lax.slice_in_dim(block, block.shape[dim] - width, None, axis=dim), axis, forward
        )
        high = lax.ppermute(lax.slice_in_dim(block, 0, width, axis=dim), axis, backward)
        block = jnp.concatenate([low, block, high], axis=dim)
    return block


def banded(taps, count, reach):
    taps = taps / jnp.sum(taps)
    rows = jnp.arange(count)[:, None]
    cols = jnp.arange(count)[None, :]
    offset = cols - rows
    where_in = jnp.abs(offset) <= reach
    index = jnp.clip(offset + reach, 0, 2 * reach)
    return jnp.where(where_in, jnp.take(taps, index), jnp.float32(0.0))


def local_axial(taps, planes_dev, reach, flipped):
    taps = taps / jnp.sum(taps)
    rows = jnp.arange(planes_dev)[:, None]
    cols = jnp.arange(planes_dev + 2 * reach)[None, :]
    if flipped:
        offset = rows + reach - cols
    else:
        offset = cols - reach - rows
    where_in = jnp.abs(offset) <= reach
    index = jnp.clip(offset + reach, 0, 2 * reach)
    return jnp.where(where_in, jnp.take(taps, index), jnp.float32(0.0))


def local(estimate, views, axial_taps, lateral_taps, cover):
    hi = lax.Precision.HIGHEST
    planes_dev, rows_all, cols_all = estimate.shape
    ky = banded(lateral_taps[0, 0], rows_all, RAD)
    kx = banded(lateral_taps[0, 1], cols_all, RAD)
    planes = lax.axis_index("blk") * planes_dev + jnp.arange(planes_dev)
    inside = (planes >= cover[0, 0]) & (planes < cover[0, 1])
    recorded = views[0]
    kz_ahead = local_axial(axial_taps[0], planes_dev, RZ, False)
    kz_behind = local_axial(axial_taps[0], planes_dev, RZ, True)
    for step in range(ITERS):
        widened = padded(estimate, (("blk", 0),), RZ)
        blurred = jnp.einsum("wc,cyx->wyx", kz_ahead, widened, precision=hi)
        blurred = jnp.einsum("zyx,wx->zyw", blurred, kx, precision=hi)
        blurred = jnp.einsum("zyx,wy->zwx", blurred, ky, precision=hi)
        ratio = recorded / blurred
        back = jnp.einsum("zyx,xw->zyw", ratio, kx, precision=hi)
        back = jnp.einsum("zyx,yw->zwx", back, ky, precision=hi)
        spread = padded(back, (("blk", 0),), RZ)
        returned = jnp.einsum("wc,cyx->wyx", kz_behind, spread, precision=hi)
        log_terms = jnp.where(inside[:, None, None], jnp.log(returned), jnp.float32(0.0))
        total = lax.psum(log_terms, "view")
        estimate = estimate * jnp.exp(total)
    return estimate


def solution(mesh):
    in_specs = (
        P("blk", None, None),
        P("view", "blk", None, None),
        P("view", None),
        P("view", None, None),
        P("view", None),
    )
    out_specs = P("blk", None, None)
    return jax.shard_map(local, mesh=mesh, in_specs=in_specs, out_specs=out_specs, check_vma=False)
```

profile of v0, /device:TPU:8, one launch (start us, length us, event | category | flops | bytes accessed | tf_op | source)
XLA Modules:
  0.0 520.1 jit_solution(3957215918461065242)
XLA Ops:
  6.5 4.1 collective-permute-start.1
  15.2 4.8 gather_fusion.1
  23.4 32.7 %collective-permute-done.1 = f32[16,128,256]{2,1,0:T(8,128)} collective-permute-done((f32[16,128,256]{2,1,0:T(8,128)}, f32[16,128,256]{2,1,0:T(8,128)}, u32[]{:S(2)}, u32[]{:S(2)}) %collective-permute-start.1) | collective-permute-done | bytes 2097184 | tf_op jit(solution)/shard_map/ppermute | solution.py:19
  61.1 6.6 %fusion.6 = f32[16,128,256]{2,0,1:T(8,128)S(1)} fusion(f32[48,128,256]{2,1,0:T(8,128)S(1)} %pad_maximum_fusion, f32[16,48]{1,0:T(8,128)S(1)} %reshape.365, s32[48]{0:T(128)S(1)} %iota_add_fusion), kind=kOutput, calls=%fused_computation.11 | convolution fusion | flops 301999872 | bytes 8391872 | tf_op jit(solution)/shard_map/wc,cyx->wyx/dot_general | solution.py:59
  67.6 13.7 %fusion.18 = f32[16,128,256]{2,1,0:T(8,128)S(1)} fusion(f32[16,128,256]{2,0,1:T(8,128)S(1)} %fusion.6, f32[]{:T(128)} %bitcast.55, f32[]{:T(128)} %bitcast.56, f32[]{:T(128)} %bitcast.57, f32[]{:T(128)} %bitcast.58, f32[]{:T(128)} %bitcast.59, f32[]{:T(128)} %bitcast.61, f32[]{:T(128)} %bitcast.60, f32[]{:T(128)} %bitcast.36, f32[]{:T(128)} %bitcast.38, ...), kind=kOutput, calls=%fused_computation.25 | convolution fusion | flops 1613955072 | bytes 4194372 | tf_op jit(solution)/shard_map/zyx,wx->zyw/dot_general | solution.py:60
  81.4 13.1 %fusion.76 = f32[128,16,256]{2,0,1:T(8,128)S(1)} fusion(f32[16,128,256]{2,1,0:T(8,128)S(1)} %fusion.18, f32[]{:T(128)} %bitcast.24, f32[]{:T(128)} %bitcast.25, f32[]{:T(128)} %bitcast.26, f32[]{:T(128)} %bitcast.27, f32[]{:T(128)} %bitcast.28, f32[]{:T(128)} %bitcast.30, f32[]{:T(128)} %bitcast.29, f32[]{:T(128)} %bitcast.5, f32[]{:T(128)} %bitcast.7, ...), kind=kOutput, calls=%fused_computation.88 | convolution fusion | flops 806141952 | bytes 4194372 | tf_op jit(solution)/shard_map/zyx,wy->zwx/dot_general | solution.py:61
  94.4 12.7 %fusion.13 = f32[16,128,256]{2,1,0:T(8,128)S(1)} fusion(f32[128,16,256]{2,0,1:T(8,128)S(1)} %fusion.76, f32[1,16,128,256]{3,2,1,0:T(8,128)S(1)} %copy-done.3, f32[]{:T(128)} %bitcast.55, f32[]{:T(128)} %bitcast.56, f32[]{:T(128)} %bitcast.57, f32[]{:T(128)} %bitcast.58, f32[]{:T(128)} %bitcast.59, f32[]{:T(128)} %bitcast.61, f32[]{:T(128)} %bitcast.60, ...), kind=kOutput, calls=%fused_computation.20 | convolution fusion | flops 1614479360 | bytes 6291524 | tf_op jit(solution)/shard_map/zyx,xw->zyw/dot_general | solution.py:63
  107.1 12.7 %convolution_bitcast_fusion.1 = f32[16,128,256]{2,1,0:T(8,128)S(1)} fusion(f32[16,128,256]{2,1,0:T(8,128)S(1)} %fusion.13, f32[]{:T(128)} %bitcast.24, f32[]{:T(128)} %bitcast.25, f32[]{:T(128)} %bitcast.26, f32[]{:T(128)} %bitcast.27, f32[]{:T(128)} %bitcast.28, f32[]{:T(128)} %bitcast.30, f32[]{:T(128)} %bitcast.29, f32[]{:T(128)} %bitcast.5, ...), kind=kOutput, calls=%fused_computation.32 | convolution fusion | flops 806141952 | bytes 4194372 | tf_op jit(solution)/shard_map/zyx,yw->zwx/dot_general | solution.py:64
  121.8 3.9 collective-permute-start.2
  125.9 4.8 gather_fusion
  132.5 35.3 %collective-permute-done.3 = f32[16,128,256]{2,1,0:T(8,128)} collective-permute-done((f32[16,128,256]{2,1,0:T(8,128)S(1)}, f32[16,128,256]{2,1,0:T(8,128)}, u32[]{:S(2)}, u32[]{:S(2)}) %collective-permute-start.3) | collective-permute-done | bytes 2097184 | tf_op jit(solution)/shard_map/ppermute | solution.py:19
  172.0 7.8 %log_select_fusion.1 = f32[16,128,256]{2,0,1:T(8,128)} fusion(f32[48,128,256]{2,1,0:T(8,128)S(1)} %pad_maximum_fusion.1, pred[16]{0:T(512)(128)(4,1)S(1)} %compare_and_fusion, f32[16,48]{1,0:T(8,128)S(1)} %reshape.361, s32[16]{0:T(128)S(1)} %iota_add_fusion.1), kind=kOutput, calls=%fused_computation.30 | convolution fusion | flops 302524160 | bytes 8391760 | tf_op jit(solution)/shard_map/wc,cyx->wyx/dot_general | solution.py:66
  179.9 80.9 %all-reduce.3.cloned.1.call-done = f32[16,128,256]{2,0,1:T(8,128)} async-done(((f32[16,128,256]{2,0,1:T(8,128)}), f32[16,128,256]{2,0,1:T(8,128)}) %all-reduce.3.cloned.1.call-update) | async-done | bytes 2097168 | tf_op jit(solution)/shard_map/psum | solution.py:68
  260.8 3.6 copy_multiply_fusion
  266.9 3.8 collective-permute-start.4
  270.7 41.1 %collective-permute-done.5 = f32[16,128,256]{2,0,1:T(8,128)S(1)} collective-permute-done((f32[16,128,256]{2,0,1:T(8,128)S(1)}, f32[16,128,256]{2,0,1:T(8,128)S(1)}, u32[]{:S(2)}, u32[]{:S(2)}) %collective-permute-start.5) | collective-permute-done | bytes 2097184 | tf_op jit(solution)/shard_map/ppermute | solution.py:19
  317.1 13.8 %fusion.16 = f32[16,128,256]{2,1,0:T(8,128)S(1)} fusion(f32[16,128,256]{2,0,1:T(8,128)S(1)} %fusion, f32[]{:T(128)} %bitcast.55, f32[]{:T(128)} %bitcast.56, f32[]{:T(128)} %bitcast.57, f32[]{:T(128)} %bitcast.58, f32[]{:T(128)} %bitcast.59, f32[]{:T(128)} %bitcast.61, f32[]{:T(128)} %bitcast.60, f32[]{:T(128)} %bitcast.36, f32[]{:T(128)} %bitcast.38, ...), kind=kOutput, calls=%fused_computation.23 | convolution fusion | flops 1613955072 | bytes 4194372 | tf_op jit(solution)/shard_map/zyx,wx->zyw/dot_general | solution.py:60
  330.9 12.9 %fusion.73 = f32[128,16,256]{2,0,1:T(8,128)S(1)} fusion(f32[16,128,256]{2,1,0:T(8,128)S(1)} %fusion.16, f32[]{:T(128)} %bitcast.24, f32[]{:T(128)} %bitcast.25, f32[]{:T(128)} %bitcast.26, f32[]{:T(128)} %bitcast.27, f32[]{:T(128)} %bitcast.28, f32[]{:T(128)} %bitcast.30, f32[]{:T(128)} %bitcast.29, f32[]{:T(128)} %bitcast.5, f32[]{:T(128)} %bitcast.7, ...), kind=kOutput, calls=%fused_computation.85 | convolution fusion | flops 806141952 | bytes 4194372 | tf_op jit(solution)/shard_map/zyx,wy->zwx/dot_general | solution.py:61
  343.7 12.8 %fusion.12 = f32[16,128,256]{2,1,0:T(8,128)S(1)} fusion(f32[128,16,256]{2,0,1:T(8,128)S(1)} %fusion.73, f32[1,16,128,256]{3,2,1,0:T(8,128)S(1)} %copy-done.4, f32[]{:T(128)} %bitcast.55, f32[]{:T(128)} %bitcast.56, f32[]{:T(128)} %bitcast.57, f32[]{:T(128)} %bitcast.58, f32[]{:T(128)} %bitcast.59, f32[]{:T(128)} %bitcast.61, f32[]{:T(128)} %bitcast.60, ...), kind=kOutput, calls=%fused_computation.18 | convolution fusion | flops 1614479360 | bytes 6291524 | tf_op jit(solution)/shard_map/zyx,xw->zyw/dot_general | solution.py:63
  356.5 12.9 %convolution_bitcast_fusion = f32[16,128,256]{2,1,0:T(8,128)S(1)} fusion(f32[16,128,256]{2,1,0:T(8,128)S(1)} %fusion.12, f32[]{:T(128)} %bitcast.24, f32[]{:T(128)} %bitcast.25, f32[]{:T(128)} %bitcast.26, f32[]{:T(128)} %bitcast.27, f32[]{:T(128)} %bitcast.28, f32[]{:T(128)} %bitcast.30, f32[]{:T(128)} %bitcast.29, f32[]{:T(128)} %bitcast.5, f32[]{:T(128)} %bitcast.7, ...), kind=kOutput, calls=%fused_computation.31 | convolution fusion | flops 806141952 | bytes 4194372 | tf_op jit(solution)/shard_map/zyx,yw->zwx/dot_general | solution.py:64
  371.4 3.9 collective-permute-start.6
  375.3 40.3 %collective-permute-done.7 = f32[16,128,256]{2,1,0:T(8,128)S(1)} collective-permute-done((f32[16,128,256]{2,1,0:T(8,128)S(1)}, f32[16,128,256]{2,1,0:T(8,128)S(1)}, u32[]{:S(2)}, u32[]{:S(2)}) %collective-permute-start.7) | collective-permute-done | bytes 2097184 | tf_op jit(solution)/shard_map/ppermute | solution.py:19
  418.2 7.8 %log_select_fusion = f32[16,128,256]{2,0,1:T(8,128)} fusion(f32[48,128,256]{2,1,0:T(8,128)S(1)} %pad_maximum_fusion.2, pred[16]{0:T(512)(128)(4,1)S(1)} %compare_and_fusion, f32[16,48]{1,0:T(8,128)S(1)} %reshape.361, s32[16]{0:T(128)S(1)} %iota_add_fusion.1), kind=kOutput, calls=%fused_computation.29 | convolution fusion | flops 302524160 | bytes 8391760 | tf_op jit(solution)/shard_map/wc,cyx->wyx/dot_general | solution.py:66
  426.1 82.3 %all-reduce.5.cloned.1.call-done = f32[16,128,256]{2,0,1:T(8,128)} async-done(((f32[16,128,256]{2,0,1:T(8,128)}), f32[16,128,256]{2,0,1:T(8,128)}) %all-reduce.5.cloned.1.call-update) | async-done | bytes 2097168 | tf_op jit(solution)/shard_map/psum | solution.py:68
  (46 shorter events, 38.0 us)
Async XLA Ops:
  6.5 254.3 %all-reduce.3.cloned.1.call-start = ((), (), s32[]{:S(2)}) async-start(), calls=%async_computation | async-start | bytes 4194304 | tf_op jit(solution)/shard_map/psum | solution.py:68
  6.5 49.6 %collective-permute-start.1 = (f32[16,128,256]{2,1,0:T(8,128)}, f32[16,128,256]{2,1,0:T(8,128)}, u32[]{:S(2)}, u32[]{:S(2)}) collective-permute-start(f32[16,128,256]{2,1,0:T(8,128)} %param.7), channel_id=1, source_target_pairs={{8,0},{16,8},{24,16},{32,24},{40,32},{48,40},{56,48},{64,56},{72,6... | collective-permute-start | bytes 6291464 | tf_op jit(solution)/shard_map/ppermute | solution.py:19
  10.6 47.4 %collective-permute-start = (f32[16,128,256]{2,1,0:T(8,128)}, f32[16,128,256]{2,1,0:T(8,128)}, u32[]{:S(2)}, u32[]{:S(2)}) collective-permute-start(f32[16,128,256]{2,1,0:T(8,128)} %param.7), channel_id=1, source_target_pairs={{0,8},{8,16},{16,24},{24,32},{32,40},{40,48},{48,56},{56,64},{64,7... | collective-permute-start | bytes 6291464 | tf_op jit(solution)/shard_map/ppermute | solution.py:16
  15.2 4.9 copy-start.1
  15.2 42.8 %copy-start = (f32[16,128,256]{2,1,0:T(8,128)S(1)}, f32[16,128,256]{2,1,0:T(8,128)}, u32[]{:S(2)}) copy-start(f32[16,128,256]{2,1,0:T(8,128)} %param.7) | copy-start | bytes 6291460
  81.3 13.1 %copy-start.3 = (f32[1,16,128,256]{3,2,1,0:T(8,128)S(1)}, f32[1,16,128,256]{3,2,1,0:T(8,128)}, u32[]{:S(2)}) copy-start(f32[1,16,128,256]{3,2,1,0:T(8,128)} %param.8) | copy-start | bytes 6291460
  119.9 48.0 %collective-permute-start.3 = (f32[16,128,256]{2,1,0:T(8,128)S(1)}, f32[16,128,256]{2,1,0:T(8,128)}, u32[]{:S(2)}, u32[]{:S(2)}) collective-permute-start(f32[16,128,256]{2,1,0:T(8,128)S(1)} %convolution_bitcast_fusion.1), channel_id=1, source_target_pairs={{8,0},{16,8},{24,16},{32,24},{40,32},{48,40},{56,48},{64,56},{72,6... | collective-permute-start | bytes 6291464 | tf_op jit(solution)/shard_map/ppermute | solution.py:19
  121.8 47.2 %collective-permute-start.2 = (f32[16,128,256]{2,1,0:T(8,128)S(1)}, f32[16,128,256]{2,1,0:T(8,128)}, u32[]{:S(2)}, u32[]{:S(2)}) collective-permute-start(f32[16,128,256]{2,1,0:T(8,128)S(1)} %convolution_bitcast_fusion.1), channel_id=1, source_target_pairs={{0,8},{8,16},{16,24},{24,32},{32,40},{40,48},{48,56},{56,64},{64,7... | collective-permute-start | bytes 6291464 | tf_op jit(solution)/shard_map/ppermute | solution.py:16
  125.9 4.9 copy-start.2
  179.9 328.5 %all-reduce.5.cloned.1.call-start = ((), (), s32[]{:S(2)}) async-start(), calls=%async_computation.1 | async-start | bytes 4194304 | tf_op jit(solution)/shard_map/psum | solution.py:68
  264.4 47.3 %collective-permute-start.5 = (f32[16,128,256]{2,0,1:T(8,128)S(1)}, f32[16,128,256]{2,0,1:T(8,128)S(1)}, u32[]{:S(2)}, u32[]{:S(2)}) collective-permute-start(f32[16,128,256]{2,0,1:T(8,128)S(1)} %copy_multiply_fusion), channel_id=1, source_target_pairs={{8,0},{16,8},{24,16},{32,24},{40,32},{48,40},{56,48},{64,56},{72,6... | collective-permute-start | bytes 6291464 | tf_op jit(solution)/shard_map/ppermute | solution.py:19
  266.9 47.1 %collective-permute-start.4 = (f32[16,128,256]{2,0,1:T(8,128)S(1)}, f32[16,128,256]{2,0,1:T(8,128)S(1)}, u32[]{:S(2)}, u32[]{:S(2)}) collective-permute-start(f32[16,128,256]{2,0,1:T(8,128)S(1)} %copy_multiply_fusion), channel_id=1, source_target_pairs={{0,8},{8,16},{16,24},{24,32},{32,40},{40,48},{48,56},{56,64},{64,7... | collective-permute-start | bytes 6291464 | tf_op jit(solution)/shard_map/ppermute | solution.py:16
  330.8 12.9 %copy-start.4 = (f32[1,16,128,256]{3,2,1,0:T(8,128)S(1)}, f32[1,16,128,256]{3,2,1,0:T(8,128)}, u32[]{:S(2)}) copy-start(f32[1,16,128,256]{3,2,1,0:T(8,128)} %param.8) | copy-start | bytes 6291460
  369.5 46.1 %collective-permute-start.7 = (f32[16,128,256]{2,1,0:T(8,128)S(1)}, f32[16,128,256]{2,1,0:T(8,128)S(1)}, u32[]{:S(2)}, u32[]{:S(2)}) collective-permute-start(f32[16,128,256]{2,1,0:T(8,128)S(1)} %convolution_bitcast_fusion), channel_id=1, source_target_pairs={{8,0},{16,8},{24,16},{32,24},{40,32},{48,40},{56,48},{64,56},{72,6... | collective-permute-start | bytes 6291464 | tf_op jit(solution)/shard_map/ppermute | solution.py:19
  371.4 46.1 %collective-permute-start.6 = (f32[16,128,256]{2,1,0:T(8,128)S(1)}, f32[16,128,256]{2,1,0:T(8,128)S(1)}, u32[]{:S(2)}, u32[]{:S(2)}) collective-permute-start(f32[16,128,256]{2,1,0:T(8,128)S(1)} %convolution_bitcast_fusion), channel_id=1, source_target_pairs={{0,8},{8,16},{16,24},{24,32},{32,40},{40,48},{48,56},{56,64},{64,7... | collective-permute-start | bytes 6291464 | tf_op jit(solution)/shard_map/ppermute | solution.py:16
Sparse Core Ops, SparseCore 0:
  180.0 80.7 all-reduce.2
  426.2 82.1 all-reduce.4
where the time goes:
time: 531 us; the launch traced here: 520 us
  waiting for transfers between devices  320 us (60%)
  matrix products  130 us (24%)
  starting transfers between devices  24 us (5%)
  other arithmetic  18.1 us (3%)
  local copies, waits for them, and re-layouts  14.4 us (3%)
  between operations  13.9 us (3%)
    psum x2, waiting for transfers between devices, local(): total = lax.psum(log_terms, 'view')  163 us
    ppermute x4, waiting for transfers between devices, padded(): lax.ppermute(lax.slice_in_dim(block, 0, width, axis=dim), axis, backward)  149 us
    dot_general x2, matrix products, local(): blurred = jnp.einsum('zyx,wx->zyw', blurred, kx, precision=hi)  27.5 us
    dot_general x2, matrix products, local(): blurred = jnp.einsum('zyx,wy->zwx', blurred, ky, precision=hi)  25.9 us
    dot_general x2, matrix products, local(): back = jnp.einsum('zyx,yw->zwx', back, ky, precision=hi)  25.6 us
    dot_general x2, matrix products, local(): back = jnp.einsum('zyx,xw->zyw', ratio, kx, precision=hi)  25.4 us
    dot_general x2, matrix products, local(): returned = jnp.einsum('wc,cyx->wyx', kz_behind, spread, precision=hi)  15.7 us
    ppermute x4, starting transfers between devices, padded(): lax.ppermute(lax.slice_in_dim(block, block.shape[dim] - width, None, axis...  13.6 us
  transfers between devices with their start and end apart: 10, of which 10 were waited for; matrix products, arithmetic and copies ran while one was open for 3% of the time, Pallas kernels for 0%

commit v1 on v0

--- a/solution.py
+++ b/solution.py
@@ -65,7 +65,8 @@
         spread = padded(back, (("blk", 0),), RZ)
         returned = jnp.einsum("wc,cyx->wyx", kz_behind, spread, precision=hi)
         log_terms = jnp.where(inside[:, None, None], jnp.log(returned), jnp.float32(0.0))
-        total = lax.psum(log_terms, "view")
+        parts = lax.all_gather(log_terms, "view", axis=0, tiled=False)
+        total = parts.sum(axis=0)
         estimate = estimate * jnp.exp(total)
     return estimate
 

time: 531 us -> 586 us (1.10)
  the two profiles are of different devices: /device:TPU:8 before, /device:TPU:1 now
where the time goes in v1:
time: 586 us; the launch traced here: 575 us
  waiting for transfers between devices  358 us (61%)
  matrix products  127 us (22%)
  other arithmetic  33.3 us (6%)
  starting transfers between devices  25.4 us (4%)
  local copies, waits for them, and re-layouts  17.3 us (3%)
  between operations  14 us (2%)
    all_gather x2, waiting for transfers between devices, local(): parts = lax.all_gather(log_terms, 'view', axis=0, tiled=False)  198 us
    ppermute x4, waiting for transfers between devices, padded(): lax.ppermute(lax.slice_in_dim(block, 0, width, axis=dim), axis, backward)  124 us
    ppermute x4, waiting for transfers between devices, padded(): lax.ppermute(lax.slice_in_dim(block, block.shape[dim] - width, None, axis...  35 us
    dot_general x2, matrix products, local(): blurred = jnp.einsum('zyx,wx->zyw', blurred, kx, precision=hi)  27.5 us
    dot_general x2, matrix products, local(): back = jnp.einsum('zyx,xw->zyw', ratio, kx, precision=hi)  25.5 us
    dot_general x2, matrix products, local(): blurred = jnp.einsum('zyx,wy->zwx', blurred, ky, precision=hi)  25.3 us
    dot_general x2, matrix products, local(): back = jnp.einsum('zyx,yw->zwx', back, ky, precision=hi)  25.2 us
    ppermute x4, starting transfers between devices, padded(): lax.ppermute(lax.slice_in_dim(block, block.shape[dim] - width, None, axis...  20.2 us
  transfers between devices with their start and end apart: 10, of which 10 were waited for; matrix products, arithmetic and copies ran while one was open for 3% of the time, Pallas kernels for 0%

profile of v1, /device:TPU:1, one launch (start us, length us, event | category | flops | bytes accessed | tf_op | source)
XLA Modules:
  0.0 574.7 jit_solution(11391682243901679853)
XLA Ops:
  9.4 5.4 collective-permute-start
  17.4 4.8 gather_fusion.1
  25.5 32.2 %collective-permute-done = f32[16,128,256]{2,0,1:T(8,128)} collective-permute-done((f32[16,128,256]{2,0,1:T(8,128)S(1)}, f32[16,128,256]{2,0,1:T(8,128)}, u32[]{:S(2)}, u32[]{:S(2)}) %collective-permute-start) | collective-permute-done | bytes 2097184 | tf_op jit(solution)/shard_map/ppermute | solution.py:16
  57.7 5.2 collective-permute-done.1
  62.9 4.9 fusion
  67.8 13.7 %fusion.22 = f32[16,128,256]{2,1,0:T(8,128)S(1)} fusion(f32[16,128,256]{2,0,1:T(8,128)S(1)} %fusion, f32[]{:T(128)} %bitcast.56, f32[]{:T(128)} %bitcast.57, f32[]{:T(128)} %bitcast.58, f32[]{:T(128)} %bitcast.59, f32[]{:T(128)} %bitcast.60, f32[]{:T(128)} %bitcast.62, f32[]{:T(128)} %bitcast.61, f32[]{:T(128)} %bitcast.37, f32[]{:T(128)} %bitcast.39, ...), kind=kOutput, calls=%fused_computation.28 | convolution fusion | flops 1613955072 | bytes 4194372 | tf_op jit(solution)/shard_map/zyx,wx->zyw/dot_general | solution.py:60
  81.5 12.6 %fusion.78 = f32[128,16,256]{2,0,1:T(8,128)S(1)} fusion(f32[16,128,256]{2,1,0:T(8,128)S(1)} %fusion.22, f32[]{:T(128)} %bitcast.24, f32[]{:T(128)} %bitcast.25, f32[]{:T(128)} %bitcast.26, f32[]{:T(128)} %bitcast.27, f32[]{:T(128)} %bitcast.28, f32[]{:T(128)} %bitcast.30, f32[]{:T(128)} %bitcast.29, f32[]{:T(128)} %bitcast.5, f32[]{:T(128)} %bitcast.7, ...), kind=kOutput, calls=%fused_computation.89 | convolution fusion | flops 806141952 | bytes 4194372 | tf_op jit(solution)/shard_map/zyx,wy->zwx/dot_general | solution.py:61
  94.2 12.7 %fusion.17 = f32[16,128,256]{2,1,0:T(8,128)S(1)} fusion(f32[128,16,256]{2,0,1:T(8,128)S(1)} %fusion.78, f32[1,16,128,256]{3,2,1,0:T(8,128)S(1)} %copy-done.2, f32[]{:T(128)} %bitcast.56, f32[]{:T(128)} %bitcast.57, f32[]{:T(128)} %bitcast.58, f32[]{:T(128)} %bitcast.59, f32[]{:T(128)} %bitcast.60, f32[]{:T(128)} %bitcast.62, f32[]{:T(128)} %bitcast.61, ...), kind=kOutput, calls=%fused_computation.23 | convolution fusion | flops 1614479360 | bytes 6291524 | tf_op jit(solution)/shard_map/zyx,xw->zyw/dot_general | solution.py:63
  106.9 12.5 %convolution_bitcast_fusion.1 = f32[16,128,256]{2,1,0:T(8,128)S(1)} fusion(f32[16,128,256]{2,1,0:T(8,128)S(1)} %fusion.17, f32[]{:T(128)} %bitcast.24, f32[]{:T(128)} %bitcast.25, f32[]{:T(128)} %bitcast.26, f32[]{:T(128)} %bitcast.27, f32[]{:T(128)} %bitcast.28, f32[]{:T(128)} %bitcast.30, f32[]{:T(128)} %bitcast.29, f32[]{:T(128)} %bitcast.5, ...), kind=kOutput, calls=%fused_computation.35 | convolution fusion | flops 806141952 | bytes 4194372 | tf_op jit(solution)/shard_map/zyx,yw->zwx/dot_general | solution.py:64
  120.7 5.6 collective-permute-start.2
  133.2 33.5 %collective-permute-done.3 = f32[16,128,256]{2,1,0:T(8,128)} collective-permute-done((f32[16,128,256]{2,1,0:T(8,128)S(1)}, f32[16,128,256]{2,1,0:T(8,128)}, u32[]{:S(2)}, u32[]{:S(2)}) %collective-permute-start.3) | collective-permute-done | bytes 2097184 | tf_op jit(solution)/shard_map/ppermute | solution.py:19
  170.8 7.8 %log_select_fusion.1 = f32[16,128,256]{2,0,1:T(8,128)} fusion(f32[48,128,256]{2,1,0:T(8,128)S(1)} %pad_maximum_fusion, pred[16]{0:T(512)(128)(4,1)S(1)} %compare_and_fusion, f32[16,48]{1,0:T(8,128)S(1)} %reshape.363, s32[16]{0:T(128)S(1)} %iota_add_fusion.1), kind=kOutput, calls=%fused_computation.33 | convolution fusion | flops 302524160 | bytes 8391760 | tf_op jit(solution)/shard_map/wc,cyx->wyx/dot_general | solution.py:66
  178.7 100.4 %all-gather.5.cloned.1.call-done = f32[128,128,256]{2,0,1:T(8,128)} async-done(((f32[16,128,256]{2,0,1:T(8,128)}), f32[128,128,256]{2,0,1:T(8,128)}) %all-gather.5.cloned.1.call-update) | async-done | bytes 16777232 | tf_op jit(solution)/shard_map/all_gather | solution.py:68
  279.1 9.8 %reduce_sum.52 = f32[16,128,256]{2,0,1:T(8,128)} reduce(f32[8,16,128,256]{3,1,0,2:T(8,128)} %bitcast.485, f32[]{:T(128)} %constant.28.clone.1), dimensions={0}, to_apply=%region_3.5 | reduce | flops 3670016 | bytes 18874372 | tf_op jit(solution)/shard_map/reduce_sum | solution.py:69
  298.0 43.3 %collective-permute-done.5 = f32[16,128,256]{2,0,1:T(8,128)S(1)} collective-permute-done((f32[16,128,256]{2,0,1:T(8,128)S(1)}, f32[16,128,256]{2,0,1:T(8,128)S(1)}, u32[]{:S(2)}, u32[]{:S(2)}) %collective-permute-start.5) | collective-permute-done | bytes 2097184 | tf_op jit(solution)/shard_map/ppermute | solution.py:19
  345.3 13.8 %fusion.20 = f32[16,128,256]{2,1,0:T(8,128)S(1)} fusion(f32[16,128,256]{2,0,1:T(8,128)S(1)} %fusion.6, f32[]{:T(128)} %bitcast.56, f32[]{:T(128)} %bitcast.57, f32[]{:T(128)} %bitcast.58, f32[]{:T(128)} %bitcast.59, f32[]{:T(128)} %bitcast.60, f32[]{:T(128)} %bitcast.62, f32[]{:T(128)} %bitcast.61, f32[]{:T(128)} %bitcast.37, f32[]{:T(128)} %bitcast.39, ...), kind=kOutput, calls=%fused_computation.26 | convolution fusion | flops 1613955072 | bytes 4194372 | tf_op jit(solution)/shard_map/zyx,wx->zyw/dot_general | solution.py:60
  359.1 12.6 %fusion.76 = f32[128,16,256]{2,0,1:T(8,128)S(1)} fusion(f32[16,128,256]{2,1,0:T(8,128)S(1)} %fusion.20, f32[]{:T(128)} %bitcast.24, f32[]{:T(128)} %bitcast.25, f32[]{:T(128)} %bitcast.26, f32[]{:T(128)} %bitcast.27, f32[]{:T(128)} %bitcast.28, f32[]{:T(128)} %bitcast.30, f32[]{:T(128)} %bitcast.29, f32[]{:T(128)} %bitcast.5, f32[]{:T(128)} %bitcast.7, ...), kind=kOutput, calls=%fused_computation.87 | convolution fusion | flops 806141952 | bytes 4194372 | tf_op jit(solution)/shard_map/zyx,wy->zwx/dot_general | solution.py:61
  371.8 12.8 %fusion.16 = f32[16,128,256]{2,1,0:T(8,128)S(1)} fusion(f32[128,16,256]{2,0,1:T(8,128)S(1)} %fusion.76, f32[1,16,128,256]{3,2,1,0:T(8,128)S(1)} %copy-done.3, f32[]{:T(128)} %bitcast.56, f32[]{:T(128)} %bitcast.57, f32[]{:T(128)} %bitcast.58, f32[]{:T(128)} %bitcast.59, f32[]{:T(128)} %bitcast.60, f32[]{:T(128)} %bitcast.62, f32[]{:T(128)} %bitcast.61, ...), kind=kOutput, calls=%fused_computation.21 | convolution fusion | flops 1614479360 | bytes 6291524 | tf_op jit(solution)/shard_map/zyx,xw->zyw/dot_general | solution.py:63
  384.6 12.7 %convolution_bitcast_fusion = f32[16,128,256]{2,1,0:T(8,128)S(1)} fusion(f32[16,128,256]{2,1,0:T(8,128)S(1)} %fusion.16, f32[]{:T(128)} %bitcast.24, f32[]{:T(128)} %bitcast.25, f32[]{:T(128)} %bitcast.26, f32[]{:T(128)} %bitcast.27, f32[]{:T(128)} %bitcast.28, f32[]{:T(128)} %bitcast.30, f32[]{:T(128)} %bitcast.29, f32[]{:T(128)} %bitcast.5, f32[]{:T(128)} %bitcast.7, ...), kind=kOutput, calls=%fused_computation.34 | convolution fusion | flops 806141952 | bytes 4194372 | tf_op jit(solution)/shard_map/zyx,yw->zwx/dot_general | solution.py:64
  398.6 4.9 collective-permute-start.6
  403.5 42.5 %collective-permute-done.7 = f32[16,128,256]{2,1,0:T(8,128)S(1)} collective-permute-done((f32[16,128,256]{2,1,0:T(8,128)S(1)}, f32[16,128,256]{2,1,0:T(8,128)S(1)}, u32[]{:S(2)}, u32[]{:S(2)}) %collective-permute-start.7) | collective-permute-done | bytes 2097184 | tf_op jit(solution)/shard_map/ppermute | solution.py:19
  447.6 7.8 %log_select_fusion = f32[16,128,256]{2,0,1:T(8,128)} fusion(f32[48,128,256]{2,1,0:T(8,128)S(1)} %pad_maximum_fusion.1, pred[16]{0:T(512)(128)(4,1)S(1)} %compare_and_fusion, f32[16,48]{1,0:T(8,128)S(1)} %reshape.363, s32[16]{0:T(128)S(1)} %iota_add_fusion.1), kind=kOutput, calls=%fused_computation.31 | convolution fusion | flops 302524160 | bytes 8391760 | tf_op jit(solution)/shard_map/wc,cyx->wyx/dot_general | solution.py:66
  455.4 97.6 %all-gather.7.cloned.1.call-done = f32[128,128,256]{2,0,1:T(8,128)} async-done(((f32[16,128,256]{2,0,1:T(8,128)}), f32[128,128,256]{2,0,1:T(8,128)}) %all-gather.7.cloned.1.call-update) | async-done | bytes 16777232 | tf_op jit(solution)/shard_map/all_gather | solution.py:68
  553.1 9.8 %reduce_sum.53 = f32[16,128,256]{2,0,1:T(8,128)} reduce(f32[8,16,128,256]{3,1,0,2:T(8,128)} %bitcast.486, f32[]{:T(128)} %constant.28.clone.1), dimensions={0}, to_apply=%region_4.6 | reduce | flops 3670016 | bytes 18874372 | tf_op jit(solution)/shard_map/reduce_sum | solution.py:69
  (48 shorter events, 41.8 us)
Async XLA Ops:
  6.5 9.6 %copy-start.4 = (f32[1,33]{1,0:T(1,128)S(1)}, f32[1,33]{1,0:T(1,128)}, u32[]{:S(2)}) copy-start(f32[1,33]{1,0:T(1,128)} %param.9) | copy-start | bytes 400
  6.5 272.5 %all-gather.5.cloned.1.call-start = ((), (), s32[]{:S(2)}) async-start(), calls=%async_computation | async-start | bytes 18874368 | tf_op jit(solution)/shard_map/all_gather | solution.py:68
  9.4 48.3 %collective-permute-start = (f32[16,128,256]{2,0,1:T(8,128)S(1)}, f32[16,128,256]{2,0,1:T(8,128)}, u32[]{:S(2)}, u32[]{:S(2)}) collective-permute-start(f32[16,128,256]{2,0,1:T(8,128)S(1)} %copy.16), channel_id=1, source_target_pairs={{0,8},{8,16},{16,24},{24,32},{32,40},{40,48},{48,56},{56,64},{64,7... | collective-permute-start | bytes 6291464 | tf_op jit(solution)/shard_map/ppermute | solution.py:16
  14.7 48.2 %collective-permute-start.1 = (f32[16,128,256]{2,0,1:T(8,128)S(1)}, f32[16,128,256]{2,0,1:T(8,128)}, u32[]{:S(2)}, u32[]{:S(2)}) collective-permute-start(f32[16,128,256]{2,0,1:T(8,128)S(1)} %copy.16), channel_id=1, source_target_pairs={{8,0},{16,8},{24,16},{32,24},{40,32},{48,40},{56,48},{64,56},{72,6... | collective-permute-start | bytes 6291464 | tf_op jit(solution)/shard_map/ppermute | solution.py:19
  17.4 4.9 copy-start
  81.5 12.6 %copy-start.2 = (f32[1,16,128,256]{3,2,1,0:T(8,128)S(1)}, f32[1,16,128,256]{3,2,1,0:T(8,128)}, u32[]{:S(2)}) copy-start(f32[1,16,128,256]{3,2,1,0:T(8,128)} %param.8) | copy-start | bytes 6291460
  119.4 47.3 %collective-permute-start.3 = (f32[16,128,256]{2,1,0:T(8,128)S(1)}, f32[16,128,256]{2,1,0:T(8,128)}, u32[]{:S(2)}, u32[]{:S(2)}) collective-permute-start(f32[16,128,256]{2,1,0:T(8,128)S(1)} %convolution_bitcast_fusion.1), channel_id=1, source_target_pairs={{8,0},{16,8},{24,16},{32,24},{40,32},{48,40},{56,48},{64,56},{72,6... | collective-permute-start | bytes 6291464 | tf_op jit(solution)/shard_map/ppermute | solution.py:19
  120.7 47.1 %collective-permute-start.2 = (f32[16,128,256]{2,1,0:T(8,128)S(1)}, f32[16,128,256]{2,1,0:T(8,128)}, u32[]{:S(2)}, u32[]{:S(2)}) collective-permute-start(f32[16,128,256]{2,1,0:T(8,128)S(1)} %convolution_bitcast_fusion.1), channel_id=1, source_target_pairs={{0,8},{8,16},{16,24},{24,32},{32,40},{40,48},{48,56},{56,64},{64,7... | collective-permute-start | bytes 6291464 | tf_op jit(solution)/shard_map/ppermute | solution.py:16
  126.5 4.9 copy-start.1
  178.6 374.4 %all-gather.7.cloned.1.call-start = ((), (), s32[]{:S(2)}) async-start(), calls=%async_computation.1 | async-start | bytes 18874368 | tf_op jit(solution)/shard_map/all_gather | solution.py:68
  292.4 48.9 %collective-permute-start.5 = (f32[16,128,256]{2,0,1:T(8,128)S(1)}, f32[16,128,256]{2,0,1:T(8,128)S(1)}, u32[]{:S(2)}, u32[]{:S(2)}) collective-permute-start(f32[16,128,256]{2,0,1:T(8,128)S(1)} %exponential_multiply_fusion.1), channel_id=1, source_target_pairs={{8,0},{16,8},{24,16},{32,24},{40,32},{48,40},{56,48},{64,56},{72,6... | collective-permute-start | bytes 6291464 | tf_op jit(solution)/shard_map/ppermute | solution.py:19
  293.7 48.4 %collective-permute-start.4 = (f32[16,128,256]{2,0,1:T(8,128)S(1)}, f32[16,128,256]{2,0,1:T(8,128)S(1)}, u32[]{:S(2)}, u32[]{:S(2)}) collective-permute-start(f32[16,128,256]{2,0,1:T(8,128)S(1)} %exponential_multiply_fusion.1), channel_id=1, source_target_pairs={{0,8},{8,16},{16,24},{24,32},{32,40},{40,48},{48,56},{56,64},{64,7... | collective-permute-start | bytes 6291464 | tf_op jit(solution)/shard_map/ppermute | solution.py:16
  359.1 12.7 %copy-start.3 = (f32[1,16,128,256]{3,2,1,0:T(8,128)S(1)}, f32[1,16,128,256]{3,2,1,0:T(8,128)}, u32[]{:S(2)}) copy-start(f32[1,16,128,256]{3,2,1,0:T(8,128)} %param.8) | copy-start | bytes 6291460
  397.3 48.7 %collective-permute-start.7 = (f32[16,128,256]{2,1,0:T(8,128)S(1)}, f32[16,128,256]{2,1,0:T(8,128)S(1)}, u32[]{:S(2)}, u32[]{:S(2)}) collective-permute-start(f32[16,128,256]{2,1,0:T(8,128)S(1)} %convolution_bitcast_fusion), channel_id=1, source_target_pairs={{8,0},{16,8},{24,16},{32,24},{40,32},{48,40},{56,48},{64,56},{72,6... | collective-permute-start | bytes 6291464 | tf_op jit(solution)/shard_map/ppermute | solution.py:19
  398.6 48.3 %collective-permute-start.6 = (f32[16,128,256]{2,1,0:T(8,128)S(1)}, f32[16,128,256]{2,1,0:T(8,128)S(1)}, u32[]{:S(2)}, u32[]{:S(2)}) collective-permute-start(f32[16,128,256]{2,1,0:T(8,128)S(1)} %convolution_bitcast_fusion), channel_id=1, source_target_pairs={{0,8},{8,16},{16,24},{24,32},{32,40},{40,48},{48,56},{56,64},{64,7... | collective-permute-start | bytes 6291464 | tf_op jit(solution)/shard_map/ppermute | solution.py:16
Sparse Core Ops, SparseCore 0:
  178.8 100.2 all-gather.4
  455.6 97.4 all-gather.6
